TPU v7x, 32 devices: a whole 2x2x4 slice. The times are simulated.
32 devices in a mesh: dp: 4 (over y, core), ctx: 8 (over z, x).
Axes of the slice: x: 2, y: 2, z: 4, core: 2. Of those that a mesh axis runs over, the one named last changes fastest.
Arguments:
- inputs: bfloat16 [4096, 1536], P(('dp', 'ctx')), may hold values from -24 to 24
- positions: int32 [4096], P(('dp', 'ctx')), may hold values from 0 to 1023, as said below
- query_weight: bfloat16 [1536, 1536], P(('dp', 'ctx')), may hold values from -1 to 1
- key_projection: bfloat16 [1536, 768], P(('dp', 'ctx')), may hold values from -1 to 1
- value_projection: bfloat16 [1536, 768], P(('dp', 'ctx')), may hold values from -0.15625 to 0.15625
- out_weight: bfloat16 [1536, 1536], P(('dp', 'ctx')), may hold values from -1.25 to 1.25
- gate_weight: bfloat16 [1536, 4096], P(('dp', 'ctx')), may hold values from -0.15625 to 0.15625
- up_weight: bfloat16 [1536, 4096], P(('dp', 'ctx')), may hold values from -0.15625 to 0.15625
- down_weight: bfloat16 [4096, 1536], P(('dp', 'ctx')), may hold values from -0.09375 to 0.09375
- attn_gain: bfloat16 [1536], P(('dp', 'ctx')), may hold values from 0.5 to 1.5
- mlp_gain: bfloat16 [1536], P(('dp', 'ctx')), may hold values from 0.5 to 1.5
- cotangent: bfloat16 [4096, 1536], P(('dp', 'ctx')), may hold values from -6 to 6
Outputs:
- outputs: bfloat16 [4096, 1536], P(('dp', 'ctx'))
- grad_inputs: float32 [4096, 1536], P(('dp', 'ctx'))
- grad_query: float32 [1536, 1536], P(('dp', 'ctx'))
- grad_key: float32 [1536, 768], P(('dp', 'ctx'))
- grad_value: float32 [1536, 768], P(('dp', 'ctx'))
- grad_out: float32 [1536, 1536], P(('dp', 'ctx'))
- grad_gate: float32 [1536, 4096], P(('dp', 'ctx'))
- grad_up: float32 [1536, 4096], P(('dp', 'ctx'))
- grad_down: float32 [4096, 1536], P(('dp', 'ctx'))
- attn_gain_grad: float32 [1536], P(('dp', 'ctx'))
- mlp_gain_grad: float32 [1536], P(('dp', 'ctx'))
Inputs may be any that keep to these rules, and one draw needn't show every extreme that they name: Each sequence holds every position once; each device's tokens are two runs of 64 rising consecutive positions, each starting at a multiple of 64.
All inputs are finite; a program needn't handle non-finite values.
Results may differ from a plain program's by a relative error of at most 0.035.
Values may be sent and summed in bfloat16 or wider, within the bound.
No kernel may reach another device: no remote copies, remote signals or barrier semaphores. Data moves between devices by JAX's collectives and lax.ppermute only.
A program may use at most 384 MiB of HBM per device.

v0:
```python
import math

import jax
import jax.numpy as jnp
from jax import lax
from jax.sharding import PartitionSpec as P

QUERY_HEADS = 16
VALUE_HEADS = 8
HEAD_ENTRIES = 96


NORM_EPS = 1e-05
ROPE_BASE = 100000.0
BLOCKED_SCORE = -1e30


def passed_along(value, axis, by):
    size = lax.axis_size(axis)
    return lax.ppermute(value, axis, [(i, (i + by) % size) for i in range(size)])


def shortened(value):
    return jax.tree.map(lambda a: a.astype(jnp.bfloat16) if a.dtype == jnp.float32 else a, value)


def rope_tables(token_pos):
    half_width = HEAD_ENTRIES // 2
    inverse = ROPE_BASE ** (-2.0 * jnp.arange(half_width, dtype=jnp.float32) / HEAD_ENTRIES)
    angles = token_pos.astype(jnp.float32)[:, None] * inverse[None, :]
    return (jnp.cos(angles), jnp.sin(angles))


def apply_rotation(vectors, cosine_lookup, sine_lookup, rot_sign):
    half_width = vectors.shape[-1] // 2
    lower_half = vectors[..., :half_width]
    upper_half = vectors[..., half_width:]
    cosine_part = cosine_lookup[:, None, :]
    sine_part = rot_sign * sine_lookup[:, None, :]
    return jnp.concatenate(
        [
            lower_half * cosine_part - upper_half * sine_part,
            upper_half * cosine_part + lower_half * sine_part,
        ],
        axis=-1,
    )


def lifted(members):
    return tuple((member.reshape((1, member.shape[0], -1)) for member in members))


def summed_rows(members):
    return tuple((jnp.sum(member, axis=0) for member in members))


def body(
    inputs,
    positions,
    query_weight,
    key_projection,
    value_projection,
    out_weight,
    gate_weight,
    up_weight,
    down_weight,
    attn_gain,
    mlp_gain,
    cotangent,
):
    token_rows = inputs.shape[0]
    heads_per_group = QUERY_HEADS // VALUE_HEADS
    score_scale = 1.0 / math.sqrt(HEAD_ENTRIES)
    cycle_size = lax.axis_size("ctx")
    cycle_index = lax.axis_index("ctx")
    key_positions = lax.all_gather(positions, "ctx", axis=0, tiled=True)
    wq_full, wk_full, wv_full, wo_full, gain_attn_full = (
        lax.all_gather(query_weight, ("dp", "ctx"), axis=0, tiled=True),
        lax.all_gather(key_projection, ("dp", "ctx"), axis=0, tiled=True),
        lax.all_gather(value_projection, ("dp", "ctx"), axis=0, tiled=True),
        lax.all_gather(out_weight, ("dp", "ctx"), axis=0, tiled=True),
        lax.all_gather(attn_gain, ("dp", "ctx"), axis=0, tiled=True),
    )
    gain_one = gain_attn_full.astype(jnp.float32)
    input_f32 = inputs.astype(jnp.float32)
    inv_rms1 = lax.rsqrt(jnp.mean(input_f32 * input_f32, axis=1, keepdims=True) + NORM_EPS)
    normalized_attention = (input_f32 * inv_rms1 * gain_one).astype(jnp.bfloat16)
    cosine_lookup, sine_lookup = rope_tables(positions)
    query_vectors = apply_rotation(
        jnp.dot(normalized_attention, wq_full, preferred_element_type=jnp.float32).reshape(
            token_rows, QUERY_HEADS, HEAD_ENTRIES
        ),
        cosine_lookup,
        sine_lookup,
        1.0,
    ).astype(jnp.bfloat16)
    query_split = query_vectors.reshape(token_rows, VALUE_HEADS, heads_per_group, HEAD_ENTRIES)
    key_matrix_rows = (
        apply_rotation(
            jnp.dot(normalized_attention, wk_full, preferred_element_type=jnp.float32).reshape(
                token_rows, VALUE_HEADS, HEAD_ENTRIES
            ),
            cosine_lookup,
            sine_lookup,
            1.0,
        )
        .astype(jnp.bfloat16)
        .reshape(token_rows, VALUE_HEADS * HEAD_ENTRIES)
    )
    value_matrix_rows = jnp.dot(
        normalized_attention, wv_full, preferred_element_type=jnp.float32
    ).astype(jnp.bfloat16)
    key_prev, value_prev = passed_along((key_matrix_rows, value_matrix_rows), "ctx", 1)
    paired_keys = jnp.stack([key_matrix_rows, key_prev])
    paired_values = jnp.stack([value_matrix_rows, value_prev])

    def tile_inputs(cycle_turn, paired_keys, paired_values):
        block_first = (cycle_index - 2 * cycle_turn) % cycle_size
        block_second = (block_first - 1) % cycle_size
        key_pos = jnp.concatenate(
            [
                lax.dynamic_slice_in_dim(key_positions, block_first * token_rows, token_rows),
                lax.dynamic_slice_in_dim(key_positions, block_second * token_rows, token_rows),
            ]
        )
        visible = key_pos[None, :] <= positions[:, None]
        return (
            visible,
            paired_keys.reshape(2 * token_rows, VALUE_HEADS, HEAD_ENTRIES),
            paired_values.reshape(2 * token_rows, VALUE_HEADS, HEAD_ENTRIES),
        )

    def forward_update(run_state, visible, key_tile, value_tile):
        top_old, total_old, accum_old = run_state
        scores = (
            jnp.einsum("qgjd,kgd->gjqk", query_split, key_tile, preferred_element_type=jnp.float32)
            * score_scale
        )
        scores = jnp.where(visible, scores, BLOCKED_SCORE)
        row_top = jnp.maximum(top_old, jnp.max(scores, axis=-1))
        probs = jnp.where(visible, jnp.exp(scores - row_top[..., None]), 0.0)
        factor = jnp.exp(top_old - row_top)
        row_total = total_old * factor + jnp.sum(probs, axis=-1)
        accum_new = accum_old * factor[..., None] + jnp.einsum(
            "gjqk,kgd->gjqd",
            probs.astype(jnp.bfloat16),
            value_tile,
            preferred_element_type=jnp.float32,
        )
        return (row_top, row_total, accum_new)

    def forward_turn(cycle_turn, loop_carry):
        run_state, paired_keys, paired_values = loop_carry
        visible, key_tile, value_tile = tile_inputs(cycle_turn, paired_keys, paired_values)
        run_state = forward_update(run_state, visible, key_tile, value_tile)
        paired_keys, paired_values = passed_along((paired_keys, paired_values), "ctx", 2)
        return (run_state, paired_keys, paired_values)

    start_state = (
        jnp.full((VALUE_HEADS, heads_per_group, token_rows), BLOCKED_SCORE, jnp.float32),
        jnp.zeros((VALUE_HEADS, heads_per_group, token_rows), jnp.float32),
        jnp.zeros((VALUE_HEADS, heads_per_group, token_rows, HEAD_ENTRIES), jnp.float32),
    )
    run_state, paired_keys, paired_values = lax.fori_loop(
        0, cycle_size // 2, forward_turn, (start_state, paired_keys, paired_values)
    )
    row_top, row_total, accum_out = run_state
    log_total = row_top + jnp.log(row_total)
    attn_four = jnp.transpose(accum_out / row_total[..., None], (2, 0, 1, 3)).astype(jnp.bfloat16)
    attention_rows = attn_four.reshape(token_rows, QUERY_HEADS * HEAD_ENTRIES)
    residual = input_f32 + jnp.dot(attention_rows, wo_full, preferred_element_type=jnp.float32)
    wg_full, wu_full, wd_full, gain_mlp_full = (
        lax.all_gather(gate_weight, ("dp", "ctx"), axis=0, tiled=True),
        lax.all_gather(up_weight, ("dp", "ctx"), axis=0, tiled=True),
        lax.all_gather(down_weight, ("dp", "ctx"), axis=0, tiled=True),
        lax.all_gather(mlp_gain, ("dp", "ctx"), axis=0, tiled=True),
    )
    gain_two = gain_mlp_full.astype(jnp.float32)
    inv_rms2 = lax.rsqrt(jnp.mean(residual * residual, axis=1, keepdims=True) + NORM_EPS)
    normed_mlp = (residual * inv_rms2 * gain_two).astype(jnp.bfloat16)
    gate_proj = jnp.dot(normed_mlp, wg_full, preferred_element_type=jnp.float32)
    up_proj = jnp.dot(normed_mlp, wu_full, preferred_element_type=jnp.float32)
    gate_sigmoid = jax.nn.sigmoid(gate_proj)
    hidden_act = (gate_proj * gate_sigmoid * up_proj).astype(jnp.bfloat16)
    outputs = (residual + jnp.dot(hidden_act, wd_full, preferred_element_type=jnp.float32)).astype(
        jnp.bfloat16
    )
    wg_back, wu_back, wd_back, gain_unused = (
        lax.all_gather(gate_weight, ("dp", "ctx"), axis=0, tiled=True),
        lax.all_gather(up_weight, ("dp", "ctx"), axis=0, tiled=True),
        lax.all_gather(down_weight, ("dp", "ctx"), axis=0, tiled=True),
        lax.all_gather(mlp_gain, ("dp", "ctx"), axis=0, tiled=True),
    )
    d_act = jnp.dot(cotangent, wd_back.T, preferred_element_type=jnp.float32)
    grad_down = jnp.dot(hidden_act.T, cotangent, preferred_element_type=jnp.float32)
    d_gate = (d_act * up_proj * gate_sigmoid * (1.0 + gate_proj * (1.0 - gate_sigmoid))).astype(
        jnp.bfloat16
    )
    d_up = (d_act * gate_proj * gate_sigmoid).astype(jnp.bfloat16)
    grad_gate = jnp.dot(normed_mlp.T, d_gate, preferred_element_type=jnp.float32)
    grad_up = jnp.dot(normed_mlp.T, d_up, preferred_element_type=jnp.float32)
    d_normed_mlp = jnp.dot(d_gate, wg_back.T, preferred_element_type=jnp.float32) + jnp.dot(
        d_up, wu_back.T, preferred_element_type=jnp.float32
    )
    gain_two_part = jnp.sum(d_normed_mlp * residual * inv_rms2, axis=0)
    scaled_two = d_normed_mlp * gain_two
    d_residual = (
        cotangent.astype(jnp.float32)
        + inv_rms2 * scaled_two
        - residual * inv_rms2**3 * jnp.mean(scaled_two * residual, axis=1, keepdims=True)
    )
    mlp_terms = lifted((grad_gate, grad_up, grad_down, gain_two_part))
    all_parts = jax.tree.map(
        lambda part, own: part.astype(own.dtype),
        lax.all_to_all(
            shortened(mlp_terms), ("dp", "ctx"), split_axis=1, concat_axis=0, tiled=True
        ),
        mlp_terms,
    )
    grad_gate_mine, grad_up_mine, grad_down_mine, mlp_gain_mine = summed_rows(all_parts)
    mlp_gain_mine = mlp_gain_mine.reshape(-1)
    wq_back, wk_back, wv_back, wo_back, gain_again = (
        lax.all_gather(query_weight, ("dp", "ctx"), axis=0, tiled=True),
        lax.all_gather(key_projection, ("dp", "ctx"), axis=0, tiled=True),
        lax.all_gather(value_projection, ("dp", "ctx"), axis=0, tiled=True),
        lax.all_gather(out_weight, ("dp", "ctx"), axis=0, tiled=True),
        lax.all_gather(attn_gain, ("dp", "ctx"), axis=0, tiled=True),
    )
    d_res_round = d_residual.astype(jnp.bfloat16)
    grad_out = jnp.dot(attention_rows.T, d_res_round, preferred_element_type=jnp.float32)
    attention_gradient = jnp.dot(d_res_round, wo_back.T, preferred_element_type=jnp.float32).astype(
        jnp.bfloat16
    )
    attention_gradient_split = attention_gradient.reshape(
        token_rows, VALUE_HEADS, heads_per_group, HEAD_ENTRIES
    )
    row_difference = jnp.transpose(
        jnp.sum(
            attention_gradient_split.astype(jnp.float32) * attn_four.astype(jnp.float32), axis=-1
        ),
        (1, 2, 0),
    )

    def backward_update(grad_state, visible, key_tile, value_tile):
        dq_accum, key_gradient_pair, value_gradient_pair = grad_state
        scores = (
            jnp.einsum("qgjd,kgd->gjqk", query_split, key_tile, preferred_element_type=jnp.float32)
            * score_scale
        )
        probs_back = jnp.where(
            visible, jnp.exp(jnp.where(visible, scores, BLOCKED_SCORE) - log_total[..., None]), 0.0
        )
        value_gradient_piece = jnp.einsum(
            "gjqk,qgjd->kgd",
            probs_back.astype(jnp.bfloat16),
            attention_gradient_split,
            preferred_element_type=jnp.float32,
        )
        d_probs = jnp.einsum(
            "qgjd,kgd->gjqk",
            attention_gradient_split,
            value_tile,
            preferred_element_type=jnp.float32,
        )
        d_scores = (score_scale * probs_back * (d_probs - row_difference[..., None])).astype(
            jnp.bfloat16
        )
        dq_accum = dq_accum + jnp.einsum(
            "gjqk,kgd->qgjd", d_scores, key_tile, preferred_element_type=jnp.float32
        )
        key_gradient_piece = jnp.einsum(
            "gjqk,qgjd->kgd", d_scores, query_split, preferred_element_type=jnp.float32
        )
        return (
            dq_accum,
            key_gradient_pair
            + key_gradient_piece.reshape(2, token_rows, VALUE_HEADS * HEAD_ENTRIES),
            value_gradient_pair
            + value_gradient_piece.reshape(2, token_rows, VALUE_HEADS * HEAD_ENTRIES),
        )

    def backward_turn(cycle_turn, loop_carry):
        grad_state, paired_keys, paired_values = loop_carry
        visible, key_tile, value_tile = tile_inputs(cycle_turn, paired_keys, paired_values)
        grad_state = backward_update(grad_state, visible, key_tile, value_tile)
        dq_accum, key_gradient_pair, value_gradient_pair = grad_state
        paired_keys, paired_values = passed_along((paired_keys, paired_values), "ctx", 2)
        key_gradient_pair, value_gradient_pair = (
            passed_along(key_gradient_pair.astype(jnp.bfloat16), "ctx", 2).astype(
                key_gradient_pair.dtype
            ),
            passed_along(value_gradient_pair.astype(jnp.bfloat16), "ctx", 2).astype(
                value_gradient_pair.dtype
            ),
        )
        return ((dq_accum, key_gradient_pair, value_gradient_pair), paired_keys, paired_values)

    empty_pair = jnp.zeros((2, token_rows, VALUE_HEADS * HEAD_ENTRIES), jnp.float32)
    initial_gradients = (
        jnp.zeros((token_rows, VALUE_HEADS, heads_per_group, HEAD_ENTRIES), jnp.float32),
        empty_pair,
        empty_pair,
    )
    grad_state, paired_keys, paired_values = lax.fori_loop(
        0, cycle_size // 2, backward_turn, (initial_gradients, paired_keys, paired_values)
    )
    dq_accum, key_gradient_pair, value_gradient_pair = grad_state
    dk_back, dv_back = (
        passed_along(key_gradient_pair[1].astype(jnp.bfloat16), "ctx", -1).astype(jnp.float32),
        passed_along(value_gradient_pair[1].astype(jnp.bfloat16), "ctx", -1).astype(jnp.float32),
    )
    key_gradient = key_gradient_pair[0] + dk_back
    value_gradient = value_gradient_pair[0] + dv_back
    dq_rot = (
        apply_rotation(
            dq_accum.reshape(token_rows, QUERY_HEADS, HEAD_ENTRIES),
            cosine_lookup,
            sine_lookup,
            -1.0,
        )
        .astype(jnp.bfloat16)
        .reshape(token_rows, QUERY_HEADS * HEAD_ENTRIES)
    )
    key_gradient_rotated = (
        apply_rotation(
            key_gradient.reshape(token_rows, VALUE_HEADS, HEAD_ENTRIES),
            cosine_lookup,
            sine_lookup,
            -1.0,
        )
        .astype(jnp.bfloat16)
        .reshape(token_rows, VALUE_HEADS * HEAD_ENTRIES)
    )
    value_gradient_rounded = value_gradient.astype(jnp.bfloat16)
    grad_query = jnp.dot(normalized_attention.T, dq_rot, preferred_element_type=jnp.float32)
    grad_key = jnp.dot(
        normalized_attention.T, key_gradient_rotated, preferred_element_type=jnp.float32
    )
    grad_value = jnp.dot(
        normalized_attention.T, value_gradient_rounded, preferred_element_type=jnp.float32
    )
    d_normed_attn = (
        jnp.dot(dq_rot, wq_back.T, preferred_element_type=jnp.float32)
        + jnp.dot(key_gradient_rotated, wk_back.T, preferred_element_type=jnp.float32)
        + jnp.dot(value_gradient_rounded, wv_back.T, preferred_element_type=jnp.float32)
    )
    gain_one_part = jnp.sum(d_normed_attn * input_f32 * inv_rms1, axis=0)
    scaled_one = d_normed_attn * gain_one
    grad_inputs = (
        d_residual
        + inv_rms1 * scaled_one
        - input_f32 * inv_rms1**3 * jnp.mean(scaled_one * input_f32, axis=1, keepdims=True)
    )
    attn_terms = lifted((grad_query, grad_key, grad_value, grad_out, gain_one_part))
    all_parts_attn = jax.tree.map(
        lambda part, own: part.astype(own.dtype),
        lax.all_to_all(
            shortened(attn_terms), ("dp", "ctx"), split_axis=1, concat_axis=0, tiled=True
        ),
        attn_terms,
    )
    grad_query_mine, grad_key_mine, grad_value_mine, grad_out_mine, attn_gain_mine = summed_rows(
        all_parts_attn
    )
    attn_gain_mine = attn_gain_mine.reshape(-1)
    return (
        outputs,
        grad_inputs,
        grad_query_mine,
        grad_key_mine,
        grad_value_mine,
        grad_out_mine,
        grad_gate_mine,
        grad_up_mine,
        grad_down_mine,
        attn_gain_mine,
        mlp_gain_mine,
    )


def solution(mesh):
    placed = (
        P(("dp", "ctx"), None),
        P(("dp", "ctx")),
        P(("dp", "ctx"), None),
        P(("dp", "ctx"), None),
        P(("dp", "ctx"), None),
        P(("dp", "ctx"), None),
        P(("dp", "ctx"), None),
        P(("dp", "ctx"), None),
        P(("dp", "ctx"), None),
        P(("dp", "ctx")),
        P(("dp", "ctx")),
        P(("dp", "ctx"), None),
    )
    return jax.shard_map(
        body,
        mesh=mesh,
        in_specs=placed,
        out_specs=(
            P(("dp", "ctx"), None),
            P(("dp", "ctx"), None),
            P(("dp", "ctx"), None),
            P(("dp", "ctx"), None),
            P(("dp", "ctx"), None),
            P(("dp", "ctx"), None),
            P(("dp", "ctx"), None),
            P(("dp", "ctx"), None),
            P(("dp", "ctx"), None),
            P(("dp", "ctx")),
            P(("dp", "ctx")),
        ),
        check_vma=False,
    )
```

profile of v0, /device:TPU:4, one launch (start us, length us, event | category | flops | bytes accessed | tf_op | source)
XLA Modules:
  0.0 2311.8 jit_solution(3486455154517269955)
XLA Ops:
  13.6 41.5 %all-reduce.2 = (bf16[1536]{0:T(1024)(128)(2,1)S(1)}, bf16[1536]{0:T(1024)(128)(2,1)S(1)}) all-reduce(bf16[1536]{0:T(1024)(128)(2,1)S(1)} %dynamic-update-slice, bf16[1536]{0:T(1024)(128)(2,1)S(1)} %dynamic-update-slice.1), channel_id=1, replica_groups=mesh['dp'=4,'ctx'=8] {'dp','ctx'}, use_global_device_ids=true, to_apply=%add | all-reduce | flops 3072 | bytes 12288
  73.0 55.3 %all-gather.11.cloned.1.call-done = bf16[1536,768]{1,0:T(8,128)(2,1)} async-done(((bf16[48,768]{1,0:T(8,128)(2,1)}), bf16[1536,768]{1,0:T(8,128)(2,1)}) %all-gather.11.cloned.1.call-update) | async-done | bytes 2359312 | tf_op jit(solution)/shard_map/all_gather | solution.py:80
  153.1 40.7 %all-gather.13.cloned.1.call-done = bf16[1536,1536]{1,0:T(8,128)(2,1)} async-done(((bf16[48,1536]{1,0:T(8,128)(2,1)}), bf16[1536,1536]{1,0:T(8,128)(2,1)}) %all-gather.13.cloned.1.call-update) | async-done | bytes 4718608 | tf_op jit(solution)/shard_map/all_gather | solution.py:78
  198.3 114.0 %while.48 = (s32[]{:T(128)}, f32[8,2,128]{2,1,0:T(2,128)S(1)}, f32[8,2,128]{2,1,0:T(2,128)S(1)}, f32[8,2,128,96]{2,3,1,0:T(8,128)}, bf16[2,128,768]{1,0,2:T(2,12...) while((s32[]{:T(128)}, f32[8,2,128]{2,1,0:T(2,128)S(1)}, ...), condition=%wide.region_4.5_spmd.clone, body=%wide.region_1.4_spmd.clone.sunk | while | flops 208775456 | bytes 15603811 | solution.py:164
  318.2 65.4 %all-gather.17.cloned.1.call-done = bf16[1536,4096]{1,0:T(8,128)(2,1)} async-done(((bf16[48,4096]{1,0:T(8,128)(2,1)}), bf16[1536,4096]{1,0:T(8,128)(2,1)}) %all-gather.17.cloned.1.call-update) | async-done | bytes 12582928 | tf_op jit(solution)/shard_map/all_gather | solution.py:173
  391.3 88.9 %all-gather.19.cloned.1.call-done = bf16[1536,4096]{1,0:T(8,128)(2,1)} async-done(((bf16[48,4096]{1,0:T(8,128)(2,1)}), bf16[1536,4096]{1,0:T(8,128)(2,1)}) %all-gather.19.cloned.1.call-update) | async-done | bytes 12582928 | tf_op jit(solution)/shard_map/all_gather | solution.py:174
  487.9 89.1 %all-gather.21.cloned.1.call-done = bf16[4096,1536]{1,0:T(8,128)(2,1)} async-done(((bf16[128,1536]{1,0:T(8,128)(2,1)}), bf16[4096,1536]{1,0:T(8,128)(2,1)}) %all-gather.21.cloned.1.call-update) | async-done | bytes 12582928 | tf_op jit(solution)/shard_map/all_gather | solution.py:175
  615.6 206.2 %while.49 = (s32[]{:T(128)}, f32[128,8,2,96]{0,3,2,1:T(8,128)}, f32[2,128,768]{1,0,2:T(2,128)}, f32[2,128,768]{1,0,2:T(2,128)}, bf16[2,128,768]{1,0,2:T(2,128)(2...) while((s32[]{:T(128)}, f32[128,8,2,96]{0,3,2,1:T(8,128)}, ...), condition=%wide.region_9.10_spmd.clone, body=%wide.region_8.9_spmd.clone.sunk | while | flops 510034208 | bytes 40622428 | solution.py:304
  863.7 33.8 %copy.113 = bf16[1,1536,768]{2,0,1:T(2,128)(2,1)} copy(bf16[1,1536,768]{2,1,0:T(8,128)(2,1)S(1)} %fusion.34) | data formatting | bytes 4718592 | tf_op jit(solution)/shard_map/convert_element_type | solution.py:24
  932.3 33.8 %copy.112 = bf16[1,1536,768]{2,0,1:T(2,128)(2,1)} copy(bf16[1,1536,768]{2,1,0:T(8,128)(2,1)S(1)} %fusion.35) | data formatting | bytes 4718592 | tf_op jit(solution)/shard_map/convert_element_type | solution.py:24
  1007.2 52.2 %copy.111 = bf16[1,1536,1536]{2,0,1:T(2,128)(2,1)} copy(bf16[1,1536,1536]{2,1,0:T(8,128)(2,1)S(1)} %fusion.32) | data formatting | bytes 9437184 | tf_op jit(solution)/shard_map/convert_element_type | solution.py:24
  1059.4 31.9 %reduce.8 = bf16[1536,1536]{1,0:T(8,128)(2,1)} reduce(bf16[1536,1,1536]{2,1,0:T(2,128)(2,1)} %bitcast.248, bf16[]{:T(256)} %broadcast.236), dimensions={1}, to_apply=%bitcast.191.reduce_sub_computation | reduce | bytes 9437186
  1107.1 52.2 %copy.110 = bf16[1,1536,1536]{2,0,1:T(2,128)(2,1)} copy(bf16[1,1536,1536]{2,1,0:T(8,128)(2,1)S(1)} %fusion.33) | data formatting | bytes 9437184 | tf_op jit(solution)/shard_map/convert_element_type | solution.py:24
  1159.3 31.9 %reduce.11 = bf16[1536,1536]{1,0:T(8,128)(2,1)} reduce(bf16[1536,1,1536]{2,1,0:T(2,128)(2,1)} %bitcast.249, bf16[]{:T(256)} %broadcast.236), dimensions={1}, to_apply=%bitcast.190.reduce_sub_computation | reduce | bytes 9437186
  1219.4 64.4 %copy.109 = bf16[1,1536,4096]{2,0,1:T(2,128)(2,1)} copy(bf16[1,1536,4096]{2,1,0:T(8,128)(2,1)S(1)} %fusion.29) | data formatting | bytes 25165824 | tf_op jit(solution)/shard_map/convert_element_type | solution.py:24
  1283.8 77.5 %reduce.12 = bf16[1536,4096]{1,0:T(8,128)(2,1)} reduce(bf16[1536,1,4096]{2,1,0:T(2,128)(2,1)} %bitcast.239, bf16[]{:T(256)} %broadcast.236), dimensions={1}, to_apply=%bitcast.189.reduce_sub_computation | reduce | bytes 25165826
  1396.2 64.4 %copy.108 = bf16[1,1536,4096]{2,0,1:T(2,128)(2,1)} copy(bf16[1,1536,4096]{2,1,0:T(8,128)(2,1)S(1)} %fusion.30) | data formatting | bytes 25165824 | tf_op jit(solution)/shard_map/convert_element_type | solution.py:24
  1460.6 77.5 %reduce.13 = bf16[1536,4096]{1,0:T(8,128)(2,1)} reduce(bf16[1536,1,4096]{2,1,0:T(2,128)(2,1)} %bitcast.240, bf16[]{:T(256)} %broadcast.236), dimensions={1}, to_apply=%bitcast.188.reduce_sub_computation | reduce | bytes 25165826
  1562.9 106.2 %all-to-all-done.4 = bf16[32,2,98304]{2,1,0:T(2,128)(2,1)} async-done(((bf16[32,2,98304]{2,1,0:T(2,128)(2,1)}), bf16[32,2,98304]{2,1,0:T(2,128)(2,1)}, u32[]{:S(2)}, u32[]{:S(2)}) %all-to-all-start.4) | async-done | bytes 12582944 | tf_op jit(solution)/shard_map/all_to_all | solution.py:215
  1685.6 137.7 %copy.107 = bf16[1,4096,1536]{2,0,1:T(2,128)(2,1)} copy(bf16[1,4096,1536]{2,1,0:T(8,128)(2,1)S(1)} %fusion.31) | data formatting | bytes 25165824 | tf_op jit(solution)/shard_map/convert_element_type | solution.py:24
  1823.2 81.0 %reduce.14 = bf16[4096,1536]{1,0:T(8,128)(2,1)} reduce(bf16[4096,1,1536]{2,1,0:T(2,128)(2,1)} %bitcast.237, bf16[]{:T(256)} %broadcast.236), dimensions={1}, to_apply=%bitcast.187.reduce_sub_computation | reduce | bytes 25165826
  1929.0 29.4 %all-to-all-done.5 = bf16[32,2,98304]{2,1,0:T(2,128)(2,1)} async-done(((bf16[32,2,98304]{2,1,0:T(2,128)(2,1)}), bf16[32,2,98304]{2,1,0:T(2,128)(2,1)}, u32[]{:S(2)}, u32[]{:S(2)}) %all-to-all-start.5) | async-done | bytes 12582944 | tf_op jit(solution)/shard_map/all_to_all | solution.py:215
  2139.0 29.4 %copy.97 = f32[1,1536,4096]{2,1,0:T(8,128)} copy(bf16[1,1536,4096]{2,0,1:T(2,128)(2,1)} %bitcast.241) | data formatting | bytes 37748736
  2205.8 29.6 %copy.98 = f32[1,1536,4096]{2,1,0:T(8,128)} copy(bf16[1,1536,4096]{2,0,1:T(2,128)(2,1)} %bitcast.243) | data formatting | bytes 37748736
  (444 shorter events, 982.0 us)
Async XLA Ops:
  7.2 62.2 %all-gather.9.cloned.1.call-start = ((), (), s32[]{:S(2)}) async-start(), calls=%async_computation.9 | async-start | bytes 2433024 | tf_op jit(solution)/shard_map/all_gather | solution.py:79
  7.9 120.4 %all-gather.11.cloned.1.call-start = ((), (), s32[]{:S(2)}) async-start(), calls=%async_computation.10 | async-start | bytes 2433024 | tf_op jit(solution)/shard_map/all_gather | solution.py:80
  8.7 185.1 %all-gather.13.cloned.1.call-start = ((), (), s32[]{:S(2)}) async-start(), calls=%async_computation.11 | async-start | bytes 4866048 | tf_op jit(solution)/shard_map/all_gather | solution.py:78
  9.4 304.3 %all-gather.15.cloned.1.call-start = ((), (), s32[]{:S(2)}) async-start(), calls=%async_computation.12 | async-start | bytes 4866048 | tf_op jit(solution)/shard_map/all_gather | solution.py:81
  10.0 373.6 %all-gather.17.cloned.1.call-start = ((), (), s32[]{:S(2)}) async-start(), calls=%async_computation.13 | async-start | bytes 12976128 | tf_op jit(solution)/shard_map/all_gather | solution.py:173
  10.6 469.7 %all-gather.19.cloned.1.call-start = ((), (), s32[]{:S(2)}) async-start(), calls=%async_computation.14 | async-start | bytes 12976128 | tf_op jit(solution)/shard_map/all_gather | solution.py:174
  11.1 565.9 %all-gather.21.cloned.1.call-start = ((), (), s32[]{:S(2)}) async-start(), calls=%async_computation.15 | async-start | bytes 12976128 | tf_op jit(solution)/shard_map/all_gather | solution.py:175
  72.3 79.6 %collective-permute-start.6 = (bf16[128,768]{1,0:T(8,128)(2,1)S(1)}, bf16[128,768]{1,0:T(8,128)(2,1)S(1)}, u32[]{:S(2)}, u32[]{:S(2)}) collective-permute-start(bf16[128,768]{1,0:T(8,128)(2,1)S(1)} %copy.61), channel_id=1, source_target_pairs={{0,1},{1,2},{2,3},{3,4},{4,5},{5,6},{6,7},{7,0},{8,9},{9,10},{10,1... | collective-permute-start | bytes 589832 | tf_op jit(solution)/shard_map/ppermute | solution.py:20
  225.4 26.4 %collective-permute-start.1 = (bf16[2,128,768]{1,0,2:T(2,128)(2,1)}, bf16[2,128,768]{1,0,2:T(2,128)(2,1)S(1)}, u32[]{:S(2)}, u32[]{:S(2)}) collective-permute-start(bf16[2,128,768]{1,0,2:T(2,128)(2,1)} %copy.127), channel_id=1, source_target_pairs={{0,2},{1,3},{2,4},{3,5},{4,6},{5,7},{6,0},{7,1},{8,10},{9,11},{10,... | collective-permute-start | bytes 1179656 | tf_op jit(solution)/shard_map/while/body/eval_jaxpr/ppermute | solution.py:20
  253.3 32.0 %collective-permute-start.1 = (bf16[2,128,768]{1,0,2:T(2,128)(2,1)}, bf16[2,128,768]{1,0,2:T(2,128)(2,1)S(1)}, u32[]{:S(2)}, u32[]{:S(2)}) collective-permute-start(bf16[2,128,768]{1,0,2:T(2,128)(2,1)} %copy.127), channel_id=1, source_target_pairs={{0,2},{1,3},{2,4},{3,5},{4,6},{5,7},{6,0},{7,1},{8,10},{9,11},{10,... | collective-permute-start | bytes 1179656 | tf_op jit(solution)/shard_map/while/body/eval_jaxpr/ppermute | solution.py:20
  636.8 31.4 %collective-permute-start.5 = (bf16[2,128,768]{1,0,2:T(2,128)(2,1)}, bf16[2,128,768]{1,0,2:T(2,128)(2,1)S(1)}, u32[]{:S(2)}, u32[]{:S(2)}) collective-permute-start(bf16[2,128,768]{1,0,2:T(2,128)(2,1)} %copy-done.8), channel_id=1, source_target_pairs={{0,2},{1,3},{2,4},{3,5},{4,6},{5,7},{6,0},{7,1},{8,10},{9,11},{10,... | collective-permute-start | bytes 1179656 | tf_op jit(solution)/shard_map/while/body/eval_jaxpr/ppermute | solution.py:20
  689.0 31.2 %collective-permute-start.5 = (bf16[2,128,768]{1,0,2:T(2,128)(2,1)}, bf16[2,128,768]{1,0,2:T(2,128)(2,1)S(1)}, u32[]{:S(2)}, u32[]{:S(2)}) collective-permute-start(bf16[2,128,768]{1,0,2:T(2,128)(2,1)} %copy-done.8), channel_id=1, source_target_pairs={{0,2},{1,3},{2,4},{3,5},{4,6},{5,7},{6,0},{7,1},{8,10},{9,11},{10,... | collective-permute-start | bytes 1179656 | tf_op jit(solution)/shard_map/while/body/eval_jaxpr/ppermute | solution.py:20
  739.7 25.6 %collective-permute-start.4 = (bf16[2,128,768]{1,0,2:T(2,128)(2,1)}, bf16[2,128,768]{1,0,2:T(2,128)(2,1)S(1)}, u32[]{:S(2)}, u32[]{:S(2)}) collective-permute-start(bf16[2,128,768]{1,0,2:T(2,128)(2,1)} %copy.144), channel_id=1, source_target_pairs={{0,2},{1,3},{2,4},{3,5},{4,6},{5,7},{6,0},{7,1},{8,10},{9,11},{10,... | collective-permute-start | bytes 1179656 | tf_op jit(solution)/shard_map/while/body/eval_jaxpr/ppermute | solution.py:20
  740.5 30.8 %collective-permute-start.5 = (bf16[2,128,768]{1,0,2:T(2,128)(2,1)}, bf16[2,128,768]{1,0,2:T(2,128)(2,1)S(1)}, u32[]{:S(2)}, u32[]{:S(2)}) collective-permute-start(bf16[2,128,768]{1,0,2:T(2,128)(2,1)} %copy-done.8), channel_id=1, source_target_pairs={{0,2},{1,3},{2,4},{3,5},{4,6},{5,7},{6,0},{7,1},{8,10},{9,11},{10,... | collective-permute-start | bytes 1179656 | tf_op jit(solution)/shard_map/while/body/eval_jaxpr/ppermute | solution.py:20
  790.9 25.5 %collective-permute-start.4 = (bf16[2,128,768]{1,0,2:T(2,128)(2,1)}, bf16[2,128,768]{1,0,2:T(2,128)(2,1)S(1)}, u32[]{:S(2)}, u32[]{:S(2)}) collective-permute-start(bf16[2,128,768]{1,0,2:T(2,128)(2,1)} %copy.144), channel_id=1, source_target_pairs={{0,2},{1,3},{2,4},{3,5},{4,6},{5,7},{6,0},{7,1},{8,10},{9,11},{10,... | collective-permute-start | bytes 1179656 | tf_op jit(solution)/shard_map/while/body/eval_jaxpr/ppermute | solution.py:20
  791.7 30.1 %collective-permute-start.5 = (bf16[2,128,768]{1,0,2:T(2,128)(2,1)}, bf16[2,128,768]{1,0,2:T(2,128)(2,1)S(1)}, u32[]{:S(2)}, u32[]{:S(2)}) collective-permute-start(bf16[2,128,768]{1,0,2:T(2,128)(2,1)} %copy-done.8), channel_id=1, source_target_pairs={{0,2},{1,3},{2,4},{3,5},{4,6},{5,7},{6,0},{7,1},{8,10},{9,11},{10,... | collective-permute-start | bytes 1179656 | tf_op jit(solution)/shard_map/while/body/eval_jaxpr/ppermute | solution.py:20
  857.0 67.3 %all-to-all-start.7 = ((bf16[1,1536,1]{2,0,1:T(2,128)(2,1)}), bf16[1,1536,1]{2,0,1:T(2,128)(2,1)}, u32[]{:S(2)}, u32[]{:S(2)}) async-start(bf16[1,1536,1]{2,0,1:T(2,128)(2,1)} %convert_element_type.417), calls=%async_computation.7 | async-start | bytes 1572864 | tf_op jit(solution)/shard_map/all_to_all | solution.py:357
  924.3 73.5 %all-to-all-start.1 = ((bf16[32,2,18432]{2,1,0:T(2,128)(2,1)}), bf16[32,2,18432]{2,1,0:T(2,128)(2,1)S(1)}, u32[]{:S(2)}, u32[]{:S(2)}) async-start(bf16[32,2,18432]{2,1,0:T(2,128)(2,1)} %reshape.398), calls=%async_computation.1 | async-start | bytes 4718592 | tf_op jit(solution)/shard_map/all_to_all | solution.py:357
  999.2 100.2 %all-to-all-start.2 = ((bf16[32,2,18432]{2,1,0:T(2,128)(2,1)}), bf16[32,2,18432]{2,1,0:T(2,128)(2,1)}, u32[]{:S(2)}, u32[]{:S(2)}) async-start(bf16[32,2,18432]{2,1,0:T(2,128)(2,1)} %reshape.400), calls=%async_computation.2 | async-start | bytes 4718592 | tf_op jit(solution)/shard_map/all_to_all | solution.py:357
  1099.5 111.2 %all-to-all-start = ((bf16[32,2,36864]{2,1,0:T(2,128)(2,1)}), bf16[32,2,36864]{2,1,0:T(2,128)(2,1)}, u32[]{:S(2)}, u32[]{:S(2)}) async-start(bf16[32,2,36864]{2,1,0:T(2,128)(2,1)} %reshape.396), calls=%async_computation | async-start | bytes 9437184 | tf_op jit(solution)/shard_map/all_to_all | solution.py:357
  1210.7 175.4 %all-to-all-start.3 = ((bf16[32,2,36864]{2,1,0:T(2,128)(2,1)}), bf16[32,2,36864]{2,1,0:T(2,128)(2,1)}, u32[]{:S(2)}, u32[]{:S(2)}) async-start(bf16[32,2,36864]{2,1,0:T(2,128)(2,1)} %reshape.402), calls=%async_computation.3 | async-start | bytes 9437184 | tf_op jit(solution)/shard_map/all_to_all | solution.py:357
  1386.0 283.0 %all-to-all-start.4 = ((bf16[32,2,98304]{2,1,0:T(2,128)(2,1)}), bf16[32,2,98304]{2,1,0:T(2,128)(2,1)}, u32[]{:S(2)}, u32[]{:S(2)}) async-start(bf16[32,2,98304]{2,1,0:T(2,128)(2,1)} %reshape.404), calls=%async_computation.4 | async-start | bytes 25165824 | tf_op jit(solution)/shard_map/all_to_all | solution.py:215
  1669.1 289.4 %all-to-all-start.5 = ((bf16[32,2,98304]{2,1,0:T(2,128)(2,1)}), bf16[32,2,98304]{2,1,0:T(2,128)(2,1)}, u32[]{:S(2)}, u32[]{:S(2)}) async-start(bf16[32,2,98304]{2,1,0:T(2,128)(2,1)} %reshape.406), calls=%async_computation.5 | async-start | bytes 25165824 | tf_op jit(solution)/shard_map/all_to_all | solution.py:215
  1958.4 289.1 %all-to-all-start.6 = ((bf16[32,2,98304]{2,1,0:T(2,128)(2,1)}), bf16[32,2,98304]{2,1,0:T(2,128)(2,1)}, u32[]{:S(2)}, u32[]{:S(2)}) async-start(bf16[32,2,98304]{2,1,0:T(2,128)(2,1)} %reshape.408), calls=%async_computation.6 | async-start | bytes 25165824 | tf_op jit(solution)/shard_map/all_to_all | solution.py:215
  (83 other events, 2804.2 us)
Sparse Core Ops, SparseCore 0:
  11.0 58.3 all-gather.8
  72.3 55.8 all-gather.10
  131.3 62.4 all-gather.12
  196.6 88.6 all-gather.14
  288.2 95.3 all-gather.16
  386.4 93.7 all-gather.18
  483.2 93.7 all-gather.20
where the time goes:
time: 2340 us; the launch traced here: 2310 us
  local copies, waits for them, and re-layouts  866 us (37%)
  waiting for transfers between devices  657 us (28%)
  other arithmetic  473 us (20%)
  matrix products  146 us (6%)
  starting transfers between devices  90.8 us (4%)
  blocking collectives  62.3 us (3%)
    convert_element_type x9, local copies, waits for them, and re-layouts, shortened(): a.astype(jnp.bfloat16)  450 us
    unnamed x114, local copies, waits for them, and re-layouts  353 us
    unnamed x13, other arithmetic  349 us
    ppermute x28, waiting for transfers between devices, passed_along(): lax.ppermute(value, axis, [(i, (i + by) % size) for i in range(size)])  153 us
    all_to_all x4, waiting for transfers between devices, body(): lax.all_to_all(shortened(mlp_terms), ('dp', 'ctx'), split_axis=1, concat_...  138 us
    all_gather x1, waiting for transfers between devices, body(): lax.all_gather(down_weight, ('dp', 'ctx'), axis=0, tiled=True)  89.1 us
    all_gather x1, waiting for transfers between devices, body(): lax.all_gather(up_weight, ('dp', 'ctx'), axis=0, tiled=True)  88.9 us
    all_gather x1, waiting for transfers between devices, body(): lax.all_gather(gate_weight, ('dp', 'ctx'), axis=0, tiled=True)  65.4 us
  transfers between devices with their start and end apart: 44, of which 34 were waited for; matrix products, arithmetic and copies ran while one was open for 58% of the time, Pallas kernels for 0%

commit v1 on v0

v1 whole, which is shorter than its diff:
```python
import math

import jax
import jax.numpy as jnp
from jax import lax
from jax.sharding import Mesh
from jax.sharding import PartitionSpec as P

QUERY_HEADS = 16
VALUE_HEADS = 8
HEAD_ENTRIES = 96
GROUP = QUERY_HEADS // VALUE_HEADS

NORM_EPS = 1e-05
ROPE_BASE = 100000.0
BLOCKED_SCORE = -1e30

BF = jnp.bfloat16
F32 = jnp.float32

ALL = ("y", "core", "r", "s", "b")
PLANE = ("y", "core", "b")
LINE = ("r", "s")
OFFSETS = tuple((y, c, b) for c in (0, 1) for y in (0, 1) for b in (0, 1))


def dot(a, b):
    return jnp.dot(a, b, preferred_element_type=F32)


def dot_tn(a, b):
    return lax.dot_general(a, b, (((0,), (0,)), ((), ())), preferred_element_type=F32)


def dot_nt(a, b):
    return lax.dot_general(a, b, (((1,), (1,)), ((), ())), preferred_element_type=F32)


def flip(value, axis):
    return lax.ppermute(value, axis, [(0, 1), (1, 0)])


def plane_pairs(first, second):
    pairs = []
    for y in (0, 1):
        for c in (0, 1):
            for b in (0, 1):
                way = first if c == 0 else second
                to = (1 - y, c, b) if way == "y" else (y, c, 1 - b)
                pairs.append(((y * 2 + c) * 2 + b, (to[0] * 2 + to[1]) * 2 + to[2]))
    return pairs


def plane_gather(own):
    core = lax.axis_index("core")
    by_b = flip(own, "b")
    by_y = flip(own, "y")
    diag = lax.ppermute(jnp.where(core == 0, by_b, by_y), PLANE, plane_pairs("y", "b"))
    return [own, by_b, by_y, diag] + [flip(v, "core") for v in (own, by_b, by_y, diag)]


def plane_scatter(parts):
    core = lax.axis_index("core")
    theirs = flip(parts[4:], "core")
    own, by_b, by_y, diag = [parts[k].astype(F32) + theirs[k].astype(F32) for k in range(4)]
    sent = jnp.stack([jnp.where(core == 0, by_b, by_y).astype(BF), diag.astype(BF)])
    got = lax.ppermute(sent, PLANE, plane_pairs("b", "y")).astype(F32)
    last = (jnp.where(core == 0, by_y, by_b) + got[1]).astype(BF)
    return own + got[0] + lax.ppermute(last, PLANE, plane_pairs("y", "b")).astype(F32)


def rope_tables(token_pos):
    half_width = HEAD_ENTRIES // 2
    inverse = ROPE_BASE ** (-2.0 * jnp.arange(half_width, dtype=F32) / HEAD_ENTRIES)
    angles = token_pos.astype(F32)[:, None] * inverse[None, :]
    return (jnp.cos(angles), jnp.sin(angles))


def apply_rotation(vectors, cosine, sine, rot_sign):
    half_width = vectors.shape[-1] // 2
    low, high = vectors[..., :half_width], vectors[..., half_width:]
    sine = rot_sign * sine
    return jnp.concatenate([low * cosine - high * sine, high * cosine + low * sine], axis=-1)


def body(sizes, inputs, positions, wq, wk, wv, wo, wg, wu, wd, attn_gain, mlp_gain, cotangent):
    D, R, S, B = sizes
    RS, T = R * S, D * B
    HE = HEAD_ENTRIES
    rows = inputs.shape[0]
    width = inputs.shape[1]
    I = wq.shape[0]
    FF = wg.shape[1]
    J = FF // (D * RS * B)
    y, core, r, s, b = [lax.axis_index(a) for a in ALL]
    dp = y * 2 + core
    scale = 1.0 / math.sqrt(HE)
    gain1 = attn_gain.astype(F32)[:, None]
    gain2 = mlp_gain.astype(F32)[:, None]

    def natural(w):
        cols = w.shape[-1]
        return w.reshape(RS, D, B * I, cols).transpose(1, 0, 2, 3).reshape(width, cols)

    def by_line(g):
        cols = g.shape[-1]
        return g.reshape(D, RS, B * I, cols).transpose(1, 0, 2, 3).reshape(width, cols)

    def to_columns(blocks):
        got = lax.all_to_all(blocks, PLANE, split_axis=0, concat_axis=0, tiled=True)
        full = lax.all_gather(got.reshape(T * I, -1), LINE, axis=0, tiled=True)
        return natural(full)

    def to_rows(grad):
        mine = lax.psum_scatter(by_line(grad).astype(BF), LINE, scatter_dimension=0, tiled=True)
        return lax.all_to_all(
            mine.reshape(T, I, -1), PLANE, split_axis=0, concat_axis=0, tiled=True
        )

    def heads_of(w, n):
        return w.reshape(I, T, n).transpose(1, 0, 2)

    def units_of(w):
        return w.reshape(I, D, RS, B, J).transpose(1, 3, 0, 2, 4).reshape(T, I, RS * J)

    def scaled(w, gain):
        return (w.astype(F32) * gain).astype(BF)

    swap = []
    for i0 in range(D):
        for ir in range(R):
            for i1 in range(S):
                for ib in range(B):
                    swap.append(
                        (((i0 * R + ir) * S + i1) * B + ib, ((i1 * R + ir) * S + i0) * B + ib)
                    )
    x_bf = lax.ppermute(inputs, ALL, swap)
    cot_bf = lax.ppermute(cotangent, ALL, swap)
    pos_all = lax.all_gather(positions, ALL, axis=0, tiled=True).reshape(D, R, T, rows)
    seats = jnp.stack([((y ^ oy) * 2 + (core ^ oc)) * B + (b ^ ob) for oy, oc, ob in OFFSETS])
    pos_seq = lax.dynamic_index_in_dim(pos_all, s, 0, keepdims=False)
    pos_seq = jnp.take(pos_seq, seats, axis=1)
    key_pos = pos_seq.reshape(-1)
    pos = lax.dynamic_index_in_dim(pos_seq, r, 0, keepdims=False).reshape(-1)
    tokens = pos.shape[0]

    qkv_blocks = jnp.concatenate(
        [heads_of(scaled(wq, gain1), GROUP * HE), heads_of(scaled(wk, gain1), HE)]
        + [heads_of(scaled(wv, gain1), HE)],
        axis=-1,
    )
    w_qkv = to_columns(qkv_blocks)
    half = RS // 2
    wo_line = lax.all_gather(wo, LINE, axis=0, tiled=True).reshape(RS, I, width)
    kept = lax.dynamic_slice_in_dim(wo_line, b * half, half)
    got = flip(lax.dynamic_slice_in_dim(wo_line, (1 - b) * half, half), "b")
    w_o = jnp.where(b == 0, jnp.stack([kept, got], 1), jnp.stack([got, kept], 1))
    w_o = w_o.reshape(GROUP * HE, width)
    w_gu = to_columns(
        jnp.concatenate([units_of(scaled(wg, gain2)), units_of(scaled(wu, gain2))], axis=-1)
    )
    w_d = lax.all_gather(wd, LINE, axis=0, tiled=True)

    x = x_bf.astype(F32)
    inv1 = lax.rsqrt(jnp.mean(x * x, axis=1, keepdims=True) + NORM_EPS)
    xh = jnp.concatenate(plane_gather((x * inv1).astype(BF)), axis=0)
    cos, sin = rope_tables(pos)
    qkv = dot(xh, w_qkv)
    q = apply_rotation(
        qkv[:, : GROUP * HE].reshape(tokens, GROUP, HE), cos[:, None], sin[:, None], 1.0
    ).astype(BF)
    k = apply_rotation(qkv[:, GROUP * HE : (GROUP + 1) * HE], cos, sin, 1.0).astype(BF)
    v = qkv[:, (GROUP + 1) * HE :].astype(BF)
    if R > 1:
        k = lax.all_gather(k, "r", axis=0, tiled=True)
        v = lax.all_gather(v, "r", axis=0, tiled=True)
    visible = key_pos[None, :] <= pos[:, None]
    scores = jnp.einsum("qjd,kd->jqk", q, k, preferred_element_type=F32) * scale
    scores = jnp.where(visible, scores, BLOCKED_SCORE)
    top = jnp.max(scores, axis=-1, keepdims=True)
    probs = jnp.where(visible, jnp.exp(scores - top), 0.0)
    total = jnp.sum(probs, axis=-1, keepdims=True)
    o = jnp.einsum("jqk,kd->jqd", probs.astype(BF), v, preferred_element_type=F32) / total
    log_total = top + jnp.log(total)
    o = jnp.transpose(o, (1, 0, 2)).astype(BF).reshape(tokens, GROUP * HE)
    residual = x + plane_scatter(dot(o, w_o).astype(BF).reshape(T, rows, width))

    cot_all = jnp.concatenate(plane_gather(cot_bf), axis=0)
    inv2 = lax.rsqrt(jnp.mean(residual * residual, axis=1, keepdims=True) + NORM_EPS)
    mh = jnp.concatenate(plane_gather((residual * inv2).astype(BF)), axis=0)
    gu = dot(mh, w_gu)
    gate, up = gu[:, : RS * J], gu[:, RS * J :]
    sig = jax.nn.sigmoid(gate)
    hidden = (gate * sig * up).astype(BF)
    d_act = dot_nt(cot_all, w_d)
    d_gate = d_act * up * sig * (1.0 + gate * (1.0 - sig))
    d_up = d_act * gate * sig
    d_gu = jnp.concatenate([d_gate.astype(BF), d_up.astype(BF)], axis=1)
    u2 = plane_scatter(dot_nt(d_gu, w_gu).astype(BF).reshape(T, rows, width))
    out_own = residual + plane_scatter(dot(hidden, w_d).astype(BF).reshape(T, rows, width))
    outputs = lax.ppermute(out_own.astype(BF), ALL, swap)
    grad_down = lax.psum_scatter(
        dot_tn(hidden, cot_all).astype(BF), LINE, scatter_dimension=0, tiled=True
    ).astype(F32)
    rows_gu = to_rows(dot_tn(mh, d_gu)).astype(F32).reshape(D, B, I, 2, RS, J)
    rows_gu = rows_gu.transpose(3, 2, 0, 4, 1, 5).reshape(2, I, FF)
    mlp_gain_grad = jnp.sum(
        rows_gu[0] * wg.astype(F32) + rows_gu[1] * wu.astype(F32), axis=1
    )
    grad_gate, grad_up = rows_gu[0] * gain2, rows_gu[1] * gain2
    d_res = (
        cot_bf.astype(F32)
        + inv2 * u2
        - residual * inv2**3 * jnp.mean(u2 * residual, axis=1, keepdims=True)
    )

    dr = jnp.concatenate(plane_gather(d_res.astype(BF)), axis=0)
    g_o = dot_tn(o, dr).astype(BF).reshape(half, B, I, width)
    g_keep = lax.dynamic_index_in_dim(g_o, b, 1, keepdims=False)
    g_got = flip(lax.dynamic_index_in_dim(g_o, 1 - b, 1, keepdims=False), "b")
    g_line = jnp.where(
        b == 0, jnp.concatenate([g_keep, g_got]), jnp.concatenate([g_got, g_keep])
    ).reshape(RS * I, width)
    grad_out = lax.psum_scatter(g_line, LINE, scatter_dimension=0, tiled=True).astype(F32)
    d_o = dot_nt(dr, w_o).astype(BF)
    d_o3, o3 = d_o.reshape(tokens, GROUP, HE), o.reshape(tokens, GROUP, HE)
    delta = jnp.sum(d_o3.astype(F32) * o3.astype(F32), axis=-1).T[..., None]
    probs_back = jnp.where(visible, jnp.exp(scores - log_total), 0.0)
    dv = jnp.einsum("jqk,qjd->kd", probs_back.astype(BF), d_o3, preferred_element_type=F32)
    d_probs = jnp.einsum("qjd,kd->jqk", d_o3, v, preferred_element_type=F32)
    d_scores = (scale * probs_back * (d_probs - delta)).astype(BF)
    dq = jnp.einsum("jqk,kd->qjd", d_scores, k, preferred_element_type=F32)
    dk = jnp.einsum("jqk,qjd->kd", d_scores, q, preferred_element_type=F32)
    if R > 1:
        dk = lax.psum_scatter(dk.astype(BF), "r", scatter_dimension=0, tiled=True).astype(F32)
        dv = lax.psum_scatter(dv.astype(BF), "r", scatter_dimension=0, tiled=True)
    dq_rot = apply_rotation(dq, cos[:, None], sin[:, None], -1.0).reshape(tokens, GROUP * HE)
    dk_rot = apply_rotation(dk, cos, sin, -1.0)
    d_qkv = jnp.concatenate([dq_rot.astype(BF), dk_rot.astype(BF), dv.astype(BF)], axis=1)
    u1 = plane_scatter(dot_nt(d_qkv, w_qkv).astype(BF).reshape(T, rows, width))
    rows_qkv = to_rows(dot_tn(xh, d_qkv)).astype(F32)
    rows_q = rows_qkv[:, :, : GROUP * HE].transpose(1, 0, 2).reshape(I, -1)
    rows_k = rows_qkv[:, :, GROUP * HE : (GROUP + 1) * HE].transpose(1, 0, 2).reshape(I, -1)
    rows_v = rows_qkv[:, :, (GROUP + 1) * HE :].transpose(1, 0, 2).reshape(I, -1)
    attn_gain_grad = (
        jnp.sum(rows_q * wq.astype(F32), axis=1)
        + jnp.sum(rows_k * wk.astype(F32), axis=1)
        + jnp.sum(rows_v * wv.astype(F32), axis=1)
    )
    gx_own = (
        d_res + inv1 * u1 - x * inv1**3 * jnp.mean(u1 * x, axis=1, keepdims=True)
    )
    grad_inputs = lax.ppermute(gx_own.astype(BF), ALL, swap).astype(F32)
    return (
        outputs,
        grad_inputs,
        rows_q * gain1,
        rows_k * gain1,
        rows_v * gain1,
        grad_out,
        grad_gate,
        grad_up,
        grad_down,
        attn_gain_grad,
        mlp_gain_grad,
    )


def solution(mesh):
    D, C = mesh.shape["dp"], mesh.shape["ctx"]
    B = VALUE_HEADS // D
    S = D
    R = C // (S * B)
    assert D == 4 and B == 2 and R * S * B == C
    fine = Mesh(mesh.devices.reshape(2, 2, R, S, B), ALL)
    wide, flat = P(ALL, None), P(ALL)

    def step(*args):
        return body((D, R, S, B), *args)

    return jax.shard_map(
        step,
        mesh=fine,
        in_specs=(wide, flat, wide, wide, wide, wide, wide, wide, wide, flat, flat, wide),
        out_specs=(wide,) * 9 + (flat, flat),
        check_vma=False,
    )
```

time: 2340 us -> 583 us (0.25)
  local copies, waits for them, and re-layouts: 866 us -> 62.9 us
  other arithmetic: 473 us -> 51.5 us
  waiting for transfers between devices: 657 us -> 238 us
  matrix products: 146 us -> 59.9 us
  starting transfers between devices: 90.8 us -> 52.5 us
  blocking collectives: 62.3 us -> 96.6 us
    convert_element_type x15 -> x2, local copies, waits for them, and re-layouts: 453 us -> 3.23 us  [to_rows(): by_line(grad).astype(BF)]
    all_gather x7 -> x3, waiting for transfers between devices: 351 us -> 0.01 us  [the longest x2 0.01 us: to_columns(): full = lax.all_gather(got.reshape(T * I, -1), LINE, axis=0, tiled=True)]
    unnamed x13 -> x3, other arithmetic: 349 us -> 2.39 us
    unnamed x114 -> x164, local copies, waits for them, and re-layouts: 353 us -> 33.6 us
    all_to_all x9 -> x4, waiting for transfers between devices: 149 us -> 0.01 us  [the longest x2 0.01 us: to_columns(): got = lax.all_to_all(blocks, PLANE, split_axis=0, concat_axis=0, tiled=True)]
    dot_general x49 -> x18, matrix products: 146 us -> 59.9 us  [the longest x4 15.6 us: dot_tn(): lax.dot_general(a, b, (((0,), (0,)), ((), ())), preferred_element_type=F32)]
    reduce_scatter x0 -> x4, waiting for transfers between devices: none -> 75.8 us  [the longest x2 75.8 us: to_rows(): lax.psum_scatter(by_line(grad).astype(BF), LINE, scatter_dimension=0, til...]
    all_gather x1 -> x2, blocking collectives: 20.9 us -> 96.6 us  [the longest x1 63.8 us: body(): lax.all_gather(positions, ALL, axis=0, tiled=True).reshape(D, R, T, rows)]
  transfers between devices with their start and end apart: 44 -> 57, of which waited for: 34 -> 20; matrix products, arithmetic and copies ran while one was open for 58% -> 25% of each run, Pallas kernels for 0% -> 0%
where the time goes in v1:
time: 583 us; the launch traced here: 577 us
  waiting for transfers between devices  238 us (41%)
  blocking collectives  96.6 us (17%)
  local copies, waits for them, and re-layouts  62.9 us (11%)
  matrix products  59.9 us (10%)
  starting transfers between devices  52.5 us (9%)
  other arithmetic  51.5 us (9%)
  between operations  15.7 us (3%)
    reduce_scatter x2, waiting for transfers between devices, to_rows(): lax.psum_scatter(by_line(grad).astype(BF), LINE, scatter_dimension=0, til...  75.8 us
    all_gather x1, blocking collectives, body(): lax.all_gather(positions, ALL, axis=0, tiled=True).reshape(D, R, T, rows)  63.8 us
    ppermute x1, waiting for transfers between devices, body(): cot_bf = lax.ppermute(cotangent, ALL, swap)  45.4 us
    ppermute x30, waiting for transfers between devices, flip(): return lax.ppermute(value, axis, [(0, 1), (1, 0)])  42.6 us
    unnamed x164, local copies, waits for them, and re-layouts  33.6 us
    all_gather x1, blocking collectives, body(): wo_line = lax.all_gather(wo, LINE, axis=0, tiled=True).reshape(RS, I, width)  32.9 us
    ppermute x4, waiting for transfers between devices, plane_scatter(): got = lax.ppermute(sent, PLANE, plane_pairs('b', 'y')).astype(F32)  26.5 us
    ppermute x1, waiting for transfers between devices, body(): outputs = lax.ppermute(out_own.astype(BF), ALL, swap)  16.9 us
  transfers between devices with their start and end apart: 57, of which 20 were waited for; matrix products, arithmetic and copies ran while one was open for 25% of the time, Pallas kernels for 0%

profile of v1, /device:TPU:4, one launch (start us, length us, event | category | flops | bytes accessed | tf_op | source)
XLA Modules:
  0.0 577.2 jit_solution(8873495684096165611)
XLA Ops:
  19.5 32.9 %all_gather.17 = bf16[192,1536]{1,0:T(8,128)(2,1)S(1)} all-gather(bf16[48,1536]{1,0:T(8,128)(2,1)S(1)} %copy-done.45), channel_id=1, replica_groups=mesh['y'=2,'core'=2,'r'=1,'s'=4,'b'=2] {'r','s'}, dimensions={0}, use_global_device_ids=true | all-gather | bytes 737280 | tf_op jit(solution)/shard_map/all_gather | solution.py:154
  55.8 63.8 %all-gather = s32[32,1,128]{2,1,0:T(1,128)S(1)} all-gather(s32[1,1,128]{2,1,0:T(1,128)S(1)} %bitcast.399), channel_id=1, replica_groups=mesh['y'=2,'core'=2,'r'=1,'s'=4,'b'=2] {'y','core','r','s','b'}, dimensions={0}, use_global_device_ids=true | all-gather | bytes 16896 | tf_op jit(solution)/shard_map/all_gather | solution.py:139
  129.8 15.7 %collective-permute-done.1 = bf16[128,1536]{1,0:T(8,128)(2,1)S(1)} collective-permute-done((bf16[128,1536]{1,0:T(8,128)(2,1)S(1)}, bf16[128,1536]{1,0:T(8,128)(2,1)S(1)}, u32[]{:S(2)}, u32[]{:S(2)}) %collective-permute-start.1) | collective-permute-done | bytes 393248 | tf_op jit(solution)/shard_map/ppermute | solution.py:40
  180.1 45.4 %collective-permute-done.23 = bf16[128,1536]{1,0:T(8,128)(2,1)S(1)} collective-permute-done((bf16[128,1536]{1,0:T(8,128)(2,1)S(1)}, bf16[128,1536]{1,0:T(8,128)(2,1)S(1)}, u32[]{:S(2)}, u32[]{:S(2)}) %collective-permute-start.23) | collective-permute-done | bytes 393248 | tf_op jit(solution)/shard_map/ppermute | solution.py:138
  228.0 7.7 %collective-permute-done.24 = bf16[128,1536]{1,0:T(8,128)(2,1)S(1)} collective-permute-done((bf16[128,1536]{1,0:T(8,128)(2,1)S(1)}, bf16[128,1536]{1,0:T(8,128)(2,1)S(1)}, u32[]{:S(2)}, u32[]{:S(2)}) %collective-permute-start.24) | collective-permute-done | bytes 393248 | tf_op jit(solution)/shard_map/ppermute | solution.py:40
  238.4 5.7 collective-permute-done.10
  249.4 5.1 collective-permute-done.11
  261.1 4.8 collective-permute-done.12
  284.2 5.2 fusion.114
  289.4 6.1 %multiply_convert_fusion.1 = (bf16[1024,512]{0,1:T(8,128)(2,1)S(1)}, bf16[1024,512]{0,1:T(8,128)(2,1)S(1)}, bf16[1024,512]{0,1:T(8,128)(2,1)S(1)}) fusion(f32[1024,1024]{0,1:T(8,128)} %fusion.114, bf16[1024,1536]{1,0:T(8,128)(2,1)} %constant_dynamic-update-slice_fusion.16, bf16[512,1536]{1,0:T(8,128)(2,1)} %all-gather.9.cloned.1.call-done), kind=kOutput, calls=%fused_computation.25 | convolution fusion | flops 1619001344 | bytes 12058624 | tf_op jit(solution)/shard_map/dot_general | solution.py:36
  307.2 8.6 %collective-permute-done.32 = bf16[2,128,1536]{2,1,0:T(8,128)(2,1)S(1)} collective-permute-done((bf16[2,128,1536]{2,1,0:T(8,128)(2,1)S(1)}, bf16[2,128,1536]{2,1,0:T(8,128)(2,1)S(1)}, u32[]{:S(2)}, u32[]{:S(2)}) %collective-permute-start.32) | collective-permute-done | bytes 786464 | tf_op jit(solution)/shard_map/ppermute | solution.py:67
  316.3 12.1 %collective-permute-done.20 = bf16[2,128,1536]{2,1,0:T(8,128)(2,1)S(1)} collective-permute-done((bf16[2,128,1536]{2,1,0:T(8,128)(2,1)S(1)}, bf16[2,128,1536]{2,1,0:T(8,128)(2,1)S(1)}, u32[]{:S(2)}, u32[]{:S(2)}) %collective-permute-start.20) | collective-permute-done | bytes 786464 | tf_op jit(solution)/shard_map/ppermute | solution.py:67
  329.0 7.8 %collective-permute-done.21 = bf16[128,1536]{1,0:T(8,128)(2,1)S(1)} collective-permute-done((bf16[128,1536]{1,0:T(8,128)(2,1)S(1)}, bf16[128,1536]{1,0:T(8,128)(2,1)S(1)}, u32[]{:S(2)}, u32[]{:S(2)}) %collective-permute-start.21) | collective-permute-done | bytes 393248 | tf_op jit(solution)/shard_map/ppermute | solution.py:69
  341.1 7.4 %collective-permute-done.34 = bf16[128,1536]{1,0:T(8,128)(2,1)} collective-permute-done((bf16[128,1536]{1,0:T(8,128)(2,1)}, bf16[128,1536]{1,0:T(8,128)(2,1)}, u32[]{:S(2)}, u32[]{:S(2)}) %collective-permute-start.34) | collective-permute-done | bytes 393248 | tf_op jit(solution)/shard_map/ppermute | solution.py:40
  353.3 5.2 convolution_convert_fusion.5
  370.8 6.1 %fusion.1 = bf16[2,1024,1024]{1,2,0:T(8,128)(2,1)S(1)} fusion(f32[1024,1024,2]{1,0,2:T(8,128)} %copy-done.2, f32[2,1024]{1,0:T(2,128)S(1)} %bitcast.398, f32[2,1024]{1,0:T(2,128)S(1)} %copy-done.53, pred[1024,1024]{0,1:T(8,128)(4,1)S(1)} %copy-done.8, bf16[1024,2,96]{0,2,1:T(8,128)(2,1)S(1)} %bitcast.391, f32[1024,384]{0,1:T(8,128)} %copy-done.28), kind=kOutput, calls=%fused_computation.3 | convolution fusion | flops 419430400 | bytes 14237696 | tf_op jit(solution)/shard_map/qjd,kd->jqk/dot_general | solution.py:230
  381.4 6.4 %fusion.18 = bf16[1024,96]{0,1:T(8,128)(2,1)S(1)} fusion(bf16[1024,2,96]{0,2,1:T(8,128)(2,1)S(1)} %bitcast.392, f32[1024,1024,2]{1,0,2:T(8,128)} %copy-done.2, f32[2,1024]{1,0:T(2,128)S(1)} %copy-done.53, pred[1024,1024]{0,1:T(8,128)(4,1)S(1)} %copy-done.8), kind=kOutput, calls=%fused_computation.39 | convolution fusion | flops 413237248 | bytes 10035200 | tf_op jit(solution)/shard_map/jqk,qjd->kd/dot_general | solution.py:229
  391.3 5.7 convolution_convert_fusion.3
  407.3 6.1 %collective-permute-start.22 = (bf16[128,1536]{1,0:T(8,128)(2,1)S(1)}, bf16[128,1536]{1,0:T(8,128)(2,1)S(1)}, u32[]{:S(2)}, u32[]{:S(2)}) collective-permute-start(bf16[128,1536]{1,0:T(8,128)(2,1)S(1)} %copy-done.40), channel_id=1, source_target_pairs={{0,0},{1,1},{2,8},{3,9},{4,16},{5,17},{6,24},{7,25},{8,2},{9,3},{1... | collective-permute-start | bytes 1179656 | tf_op jit(solution)/shard_map/ppermute | solution.py:201
  415.4 16.9 %collective-permute-done.22 = bf16[128,1536]{1,0:T(8,128)(2,1)S(1)} collective-permute-done((bf16[128,1536]{1,0:T(8,128)(2,1)S(1)}, bf16[128,1536]{1,0:T(8,128)(2,1)S(1)}, u32[]{:S(2)}, u32[]{:S(2)}) %collective-permute-start.22) | collective-permute-done | bytes 393248 | tf_op jit(solution)/shard_map/ppermute | solution.py:201
  434.2 22.5 %reduce-scatter.5.cloned.1.call-done = bf16[384,384]{1,0:T(8,128)(2,1)} async-done(((bf16[1536,384]{1,0:T(8,128)(2,1)}), bf16[384,384]{1,0:T(8,128)(2,1)}) %reduce-scatter.5.cloned.1.call-update) | async-done | bytes 294928 | tf_op jit(solution)/shard_map/reduce_scatter | solution.py:115
  464.7 53.3 %reduce-scatter.9.cloned.1.call-done = bf16[384,1024]{1,0:T(8,128)(2,1)} async-done(((bf16[1536,1024]{1,0:T(8,128)(2,1)}), bf16[384,1024]{1,0:T(8,128)(2,1)}) %reduce-scatter.9.cloned.1.call-update) | async-done | bytes 786448 | tf_op jit(solution)/shard_map/reduce_scatter | solution.py:115
  518.0 4.7 all-to-all-start.3
  555.4 12.2 %collective-permute-done.44 = bf16[128,1536]{1,0:T(8,128)(2,1)} collective-permute-done((bf16[128,1536]{1,0:T(8,128)(2,1)}, bf16[128,1536]{1,0:T(8,128)(2,1)}, u32[]{:S(2)}, u32[]{:S(2)}) %collective-permute-start.44) | collective-permute-done | bytes 393248 | tf_op jit(solution)/shard_map/ppermute | solution.py:253
  (387 shorter events, 194.2 us)
Async XLA Ops:
  11.4 109.9 %all-to-all-start = ((bf16[8,48,384]{2,1,0:T(8,128)(2,1)}), bf16[8,48,384]{2,1,0:T(8,128)(2,1)S(1)}, u32[]{:S(2)}, u32[]{:S(2)}) async-start(bf16[8,48,384]{2,1,0:T(8,128)(2,1)} %copy.56), calls=%async_computation | async-start | bytes 589824 | tf_op jit(solution)/shard_map/all_to_all | solution.py:110
  15.6 111.1 %collective-permute-start = (bf16[128,1536]{1,0:T(8,128)(2,1)}, bf16[128,1536]{1,0:T(8,128)(2,1)S(1)}, u32[]{:S(2)}, u32[]{:S(2)}) collective-permute-start(bf16[128,1536]{1,0:T(8,128)(2,1)} %param.12), channel_id=1, source_target_pairs={{0,0},{1,1},{2,8},{3,9},{4,16},{5,17},{6,24},{7,25},{8,2},{9,3},{1... | collective-permute-start | bytes 1179656 | tf_op jit(solution)/shard_map/ppermute | solution.py:137
  52.5 96.3 %collective-permute-start.8 = (bf16[2,48,1536]{2,1,0:T(8,128)(2,1)S(1)}, bf16[2,48,1536]{2,1,0:T(8,128)(2,1)}, u32[]{:S(2)}, u32[]{:S(2)}) collective-permute-start(bf16[2,48,1536]{2,1,0:T(8,128)(2,1)S(1)} %get-tuple-element.51), channel_id=1, source_target_pairs={{0,1},{1,0},{2,3},{3,2},{4,5},{5,4},{6,7},{7,6},{8,9},{9,8},{10,11... | collective-permute-start | bytes 884744 | tf_op jit(solution)/shard_map/ppermute | solution.py:40
  121.2 29.7 %all-to-all-start.1 = ((bf16[8,48,1024]{2,1,0:T(8,128)(2,1)}), bf16[8,48,1024]{2,1,0:T(8,128)(2,1)S(1)}, u32[]{:S(2)}, u32[]{:S(2)}) async-start(bf16[8,48,1024]{2,1,0:T(8,128)(2,1)} %pad_maximum_fusion.4), calls=%async_computation.1 | async-start | bytes 1572864 | tf_op jit(solution)/shard_map/all_to_all | solution.py:110
  125.9 34.5 %all-gather.5.cloned.1.call-start = ((), (), s32[]{:S(2)}) async-start(), calls=%async_computation.8 | async-start | bytes 1474560 | tf_op jit(solution)/shard_map/all_gather | solution.py:111
  126.6 146.1 %all-gather.7.cloned.1.call-start = ((), (), s32[]{:S(2)}) async-start(), calls=%async_computation.9 | async-start | bytes 3932160 | tf_op jit(solution)/shard_map/all_gather | solution.py:111
  127.5 17.9 %collective-permute-start.1 = (bf16[128,1536]{1,0:T(8,128)(2,1)S(1)}, bf16[128,1536]{1,0:T(8,128)(2,1)S(1)}, u32[]{:S(2)}, u32[]{:S(2)}) collective-permute-start(bf16[128,1536]{1,0:T(8,128)(2,1)S(1)} %get-tuple-element.21), channel_id=1, source_target_pairs={{0,1},{1,0},{2,3},{3,2},{4,5},{5,4},{6,7},{7,6},{8,9},{9,8},{10,11... | collective-permute-start | bytes 1179656 | tf_op jit(solution)/shard_map/ppermute | solution.py:40
  151.9 137.5 %all-gather.9.cloned.1.call-start = ((), (), s32[]{:S(2)}) async-start(), calls=%async_computation.10 | async-start | bytes 1966080 | tf_op jit(solution)/shard_map/all_gather | solution.py:162
  177.3 49.5 %collective-permute-start.9 = (bf16[4,128,1536]{2,1,0:T(8,128)(2,1)S(1)}, bf16[4,128,1536]{2,1,0:T(8,128)(2,1)S(1)}, u32[]{:S(2)}, u32[]{:S(2)}) collective-permute-start(bf16[4,128,1536]{2,1,0:T(8,128)(2,1)S(1)} %bitcast.375), channel_id=1, source_target_pairs={{0,8},{8,0},{1,9},{9,1},{2,10},{10,2},{3,11},{11,3},{4,12},{12,4},... | collective-permute-start | bytes 4718600 | tf_op jit(solution)/shard_map/ppermute | solution.py:40
  178.1 47.4 %collective-permute-start.23 = (bf16[128,1536]{1,0:T(8,128)(2,1)S(1)}, bf16[128,1536]{1,0:T(8,128)(2,1)S(1)}, u32[]{:S(2)}, u32[]{:S(2)}) collective-permute-start(bf16[128,1536]{1,0:T(8,128)(2,1)S(1)} %copy-done.65), channel_id=1, source_target_pairs={{0,0},{1,1},{2,8},{3,9},{4,16},{5,17},{6,24},{7,25},{8,2},{9,3},{1... | collective-permute-start | bytes 1179656 | tf_op jit(solution)/shard_map/ppermute | solution.py:138
  246.5 166.9 %reduce-scatter.11.cloned.1.call-start = ((), (), s32[]{:S(2)}) async-start(), calls=%async_computation.14 | async-start | bytes 1966080 | tf_op jit(solution)/shard_map/reduce_scatter | solution.py:202
  246.6 23.7 %collective-permute-start.29 = (bf16[128,1536]{1,0:T(8,128)(2,1)}, bf16[128,1536]{1,0:T(8,128)(2,1)S(1)}, u32[]{:S(2)}, u32[]{:S(2)}) collective-permute-start(bf16[128,1536]{1,0:T(8,128)(2,1)} %copy-done.32), channel_id=1, source_target_pairs={{0,8},{8,0},{1,9},{9,1},{2,10},{10,2},{3,11},{11,3},{4,12},{12,4},... | collective-permute-start | bytes 1179656 | tf_op jit(solution)/shard_map/ppermute | solution.py:40
  247.2 23.9 %collective-permute-start.30 = (bf16[128,1536]{1,0:T(8,128)(2,1)}, bf16[128,1536]{1,0:T(8,128)(2,1)S(1)}, u32[]{:S(2)}, u32[]{:S(2)}) collective-permute-start(bf16[128,1536]{1,0:T(8,128)(2,1)} %collective-permute-done.26), channel_id=1, source_target_pairs={{0,8},{8,0},{1,9},{9,1},{2,10},{10,2},{3,11},{11,3},{4,12},{12,4},... | collective-permute-start | bytes 1179656 | tf_op jit(solution)/shard_map/ppermute | solution.py:40
  306.8 21.7 %collective-permute-start.20 = (bf16[2,128,1536]{2,1,0:T(8,128)(2,1)S(1)}, bf16[2,128,1536]{2,1,0:T(8,128)(2,1)S(1)}, u32[]{:S(2)}, u32[]{:S(2)}) collective-permute-start(bf16[2,128,1536]{2,1,0:T(8,128)(2,1)S(1)} %pad_maximum_fusion.5), channel_id=1, source_target_pairs={{0,1},{1,0},{8,24},{9,25},{16,17},{17,16},{24,8},{25,9},{2,3},{3,2... | collective-permute-start | bytes 2359304 | tf_op jit(solution)/shard_map/ppermute | solution.py:67
  341.1 20.3 %collective-permute-start.37 = (bf16[128,1536]{1,0:T(8,128)(2,1)}, bf16[128,1536]{1,0:T(8,128)(2,1)}, u32[]{:S(2)}, u32[]{:S(2)}) collective-permute-start(bf16[128,1536]{1,0:T(8,128)(2,1)} %get-tuple-element.12), channel_id=1, source_target_pairs={{0,8},{8,0},{1,9},{9,1},{2,10},{10,2},{3,11},{11,3},{4,12},{12,4},... | collective-permute-start | bytes 1179656 | tf_op jit(solution)/shard_map/ppermute | solution.py:40
  358.5 73.9 %reduce-scatter.7.cloned.1.call-start = ((), (), s32[]{:S(2)}) async-start(), calls=%async_computation.12 | async-start | bytes 737280 | tf_op jit(solution)/shard_map/reduce_scatter | solution.py:224
  381.4 75.3 %reduce-scatter.5.cloned.1.call-start = ((), (), s32[]{:S(2)}) async-start(), calls=%async_computation.11 | async-start | bytes 1474560 | tf_op jit(solution)/shard_map/reduce_scatter | solution.py:115
  391.0 127.0 %reduce-scatter.9.cloned.1.call-start = ((), (), s32[]{:S(2)}) async-start(), calls=%async_computation.13 | async-start | bytes 3932160 | tf_op jit(solution)/shard_map/reduce_scatter | solution.py:115
  406.1 55.0 %collective-permute-start.42 = (bf16[2,128,1536]{2,1,0:T(8,128)(2,1)S(1)}, bf16[2,128,1536]{2,1,0:T(8,128)(2,1)}, u32[]{:S(2)}, u32[]{:S(2)}) collective-permute-start(bf16[2,128,1536]{2,1,0:T(8,128)(2,1)S(1)} %pad_maximum_fusion.8), channel_id=1, source_target_pairs={{0,1},{1,0},{8,24},{9,25},{16,17},{17,16},{24,8},{25,9},{2,3},{3,2... | collective-permute-start | bytes 2359304 | tf_op jit(solution)/shard_map/ppermute | solution.py:67
  407.3 25.0 %collective-permute-start.22 = (bf16[128,1536]{1,0:T(8,128)(2,1)S(1)}, bf16[128,1536]{1,0:T(8,128)(2,1)S(1)}, u32[]{:S(2)}, u32[]{:S(2)}) collective-permute-start(bf16[128,1536]{1,0:T(8,128)(2,1)S(1)} %copy-done.40), channel_id=1, source_target_pairs={{0,0},{1,1},{2,8},{3,9},{4,16},{5,17},{6,24},{7,25},{8,2},{9,3},{1... | collective-permute-start | bytes 1179656 | tf_op jit(solution)/shard_map/ppermute | solution.py:201
  456.6 61.3 %all-to-all-start.2 = ((bf16[8,48,384]{2,1,0:T(8,128)(2,1)}), bf16[8,48,384]{2,1,0:T(8,128)(2,1)}, u32[]{:S(2)}, u32[]{:S(2)}) async-start(bf16[8,48,384]{2,1,0:T(8,128)(2,1)} %bitcast.395), calls=%async_computation.3 | async-start | bytes 589824 | tf_op jit(solution)/shard_map/all_to_all | solution.py:116
  464.5 76.1 %collective-permute-start.43 = (bf16[128,1536]{1,0:T(8,128)(2,1)}, bf16[128,1536]{1,0:T(8,128)(2,1)}, u32[]{:S(2)}, u32[]{:S(2)}) collective-permute-start(bf16[128,1536]{1,0:T(8,128)(2,1)} %fusion.48), channel_id=1, source_target_pairs={{0,16},{1,17},{8,9},{9,8},{16,0},{17,1},{24,25},{25,24},{2,18},{3,... | collective-permute-start | bytes 1179656 | tf_op jit(solution)/shard_map/ppermute | solution.py:69
  518.0 30.5 %all-to-all-start.3 = ((bf16[8,48,1024]{2,1,0:T(8,128)(2,1)}), bf16[8,48,1024]{2,1,0:T(8,128)(2,1)}, u32[]{:S(2)}, u32[]{:S(2)}) async-start(bf16[8,48,1024]{2,1,0:T(8,128)(2,1)} %bitcast.386), calls=%async_computation.6 | async-start | bytes 1572864 | tf_op jit(solution)/shard_map/all_to_all | solution.py:116
  544.3 23.2 %collective-permute-start.44 = (bf16[128,1536]{1,0:T(8,128)(2,1)}, bf16[128,1536]{1,0:T(8,128)(2,1)}, u32[]{:S(2)}, u32[]{:S(2)}) collective-permute-start(bf16[128,1536]{1,0:T(8,128)(2,1)} %fusion.55), channel_id=1, source_target_pairs={{0,0},{1,1},{2,8},{3,9},{4,16},{5,17},{6,24},{7,25},{8,2},{9,3},{1... | collective-permute-start | bytes 1179656 | tf_op jit(solution)/shard_map/ppermute | solution.py:253
  (104 other events, 827.2 us)
Sparse Core Ops, SparseCore 0:
  128.8 28.3 all-gather.4
  159.4 67.4 all-gather.6
  246.6 39.1 all-gather.8
  358.6 36.2 reduce-scatter.10
  397.6 22.5 reduce-scatter.6
  422.4 34.2 reduce-scatter.4
  458.9 58.9 reduce-scatter.8
